TPU v7x, 32 devices: a whole 2x2x4 slice. The times are simulated.
32 devices in a mesh: ra: 4 (over z), dec: 8 (over y, x, core).
Axes of the slice: x: 2, y: 2, z: 4, core: 2. Of those that a mesh axis runs over, the one named last changes fastest.
Arguments:
- forests: bfloat16 [8, 32, 128, 1024], P('ra', 'dec'), may hold values from -6 to 6
- resolution: float32 [8, 32, 128], P('ra', 'dec'), may hold values from 0.3 to 1.2
- pixel_range: int32 [8, 32, 2, 128], P('ra', 'dec'), may hold values from 0 to 1024, as said below
- block_pairs: int32 [4, 8, 40, 3], P('ra', 'dec'), may hold values from -1 to 7, as said below
- block_count: int32 [4, 8], P('ra', 'dec'), may hold values from 10 to 40, as said below
- separation_bin: int32 [4, 8, 40, 128, 128], P('ra', 'dec'), may hold values from 0 to 8
Outputs:
- tile_power: float32 [4, 8, 8, 128], P('ra', 'dec')
- sky_power: float32 [8, 128], replicated
Inputs may be any that keep to these rules, and one draw needn't show every extreme that they name: `pixel_range`: lo < hi for every forest; at least 256 valid pixels. `block_pairs`: each device's list names every one of its own cells once with each of the five offsets (0, 0), (0, 1), (1, -1), (1, 0), (1, 1), in an order drawn from the seed. Slots at or past block_count are ignored. `block_count`: some device has all 40 slots live in every draw.
All inputs are finite; a program needn't handle non-finite values.
Results may differ from a plain program's by a relative error of at most 0.0037.
Values may be sent and summed in bfloat16 or wider, within the bound.
No kernel may reach another device: no remote copies, remote signals or barrier semaphores. Data moves between devices by JAX's collectives and lax.ppermute only.
A program may use at most 64 MiB of HBM per device.

v0:
```python
import jax
import jax.numpy as jnp
from jax import lax
from jax.sharding import PartitionSpec as P

NSEP = 8
NKB = 128


def extended(block, sides, width):
    for axis, dim in sides:
        count = lax.axis_size(axis)
        forward = [(i, i + 1) for i in range(count - 1)]
        backward = [(target, source) for source, target in forward]
        low = lax.ppermute(
            lax.slice_in_dim(block, block.shape[dim] - width, None, axis=dim), axis, forward
        )
        high = lax.ppermute(lax.slice_in_dim(block, 0, width, axis=dim), axis, backward)
        block = jnp.concatenate([low, block, high], axis=dim)
    return block


def from_behind(value, axis, steps):
    count = lax.axis_size(axis)
    leading, last = (max(0, -steps), min(count, count - steps))
    return lax.ppermute(value, axis, [(source, source + steps) for source in range(leading, last)])


def dft_table(length, n_modes):
    sample = jnp.arange(length, dtype=jnp.int32)[:, None]
    mode_index = jnp.arange(n_modes, dtype=jnp.int32)[None, :]
    angles = (sample * mode_index % length).astype(jnp.float32) * (2.0 * jnp.pi / length)
    return jnp.concatenate([jnp.cos(angles), jnp.sin(angles)], axis=1).astype(jnp.bfloat16)


def kbin_table(n_modes, n_bins):
    column = jnp.arange(2 * n_modes, dtype=jnp.int32) % n_modes
    which = column // (n_modes // n_bins)
    return (which[:, None] == jnp.arange(n_bins, dtype=jnp.int32)[None, :]).astype(jnp.float32)


def mask_pixels(flux, pixel_range):
    position = jnp.arange(flux.shape[-1], dtype=jnp.int32)
    lower = pixel_range[..., 0, :][..., None]
    upper = pixel_range[..., 1, :][..., None]
    inside = (position >= lower) & (position < upper)
    return jnp.where(inside, flux, jnp.zeros_like(flux))


def to_spectra(masked, widths, basis):
    length = basis.shape[0]
    n_modes = basis.shape[1] // 2
    raw = jnp.dot(masked, basis, preferred_element_type=jnp.float32)
    wavenum = jnp.arange(n_modes, dtype=jnp.float32) * (2.0 * jnp.pi / length)
    wavenum = jnp.concatenate([wavenum, wavenum])
    window = jnp.exp(-0.5 * (wavenum * widths[..., None]) ** 2)
    return (raw * window).astype(jnp.bfloat16)


def block_term(grid_flat, index_a, index_b, sep_bins):
    n_sep = NSEP
    per_cell = sep_bins.shape[0]
    left = lax.dynamic_index_in_dim(grid_flat, index_a, 0, keepdims=False)
    right = lax.dynamic_index_in_dim(grid_flat, index_b, 0, keepdims=False)
    onehot = (sep_bins[None, :, :] == jnp.arange(n_sep, dtype=jnp.int32)[:, None, None]).astype(
        jnp.bfloat16
    )
    mixed = jnp.dot(
        onehot.reshape(n_sep * per_cell, per_cell), right, preferred_element_type=jnp.float32
    )
    mixed = mixed.reshape(n_sep, per_cell, -1)
    block_sum = jnp.sum(mixed * left.astype(jnp.float32)[None], axis=1)
    pair_counts = jnp.sum(onehot.reshape(n_sep, -1).astype(jnp.float32), axis=1)
    return (block_sum, pair_counts)


def per_device(forests, resolution, pixel_range, block_pairs, block_count, separation_bin):
    cells_ra, cells_dec, per_cell, length = forests.shape
    basis = dft_table(length, length // 2)
    masked = mask_pixels(forests, pixel_range)
    own_spectra = to_spectra(masked, resolution, basis)
    sided = extended(own_spectra, (("dec", 1),), 1)
    above = from_behind(sided[0:1], "ra", -1)
    padded = jnp.concatenate([sided, above], axis=0)
    cols_pad = cells_dec + 2
    grid_flat = padded.reshape(-1, per_cell, length)
    entries = block_pairs[0, 0]
    sep_bins = separation_bin[0, 0]
    live_count = block_count[0, 0]

    def slot_term(slot_index):
        entry_row = entries[slot_index]
        row_a = entry_row[0] // cells_dec
        col_a = entry_row[0] % cells_dec + 1
        index_a = row_a * cols_pad + col_a
        index_b = (row_a + entry_row[1]) * cols_pad + col_a + entry_row[2]
        return block_term(grid_flat, index_a, index_b, sep_bins[slot_index])

    start_value = (jnp.zeros((NSEP, length), jnp.float32), jnp.zeros((NSEP,), jnp.float32))

    def add_live(slot_index, carry):
        block_sum, counts = slot_term(slot_index)
        return (carry[0] + block_sum, carry[1] + counts)

    sums, counts = lax.fori_loop(0, live_count, add_live, start_value)
    binned = jnp.dot(sums, kbin_table(length // 2, NKB), precision=lax.Precision.HIGHEST)
    tile_power = (binned / (per_cell * length)).reshape(1, 1, NSEP, NKB)
    summed, all_counts = lax.psum((binned, counts), ("ra", "dec"))
    sky_power = summed / jnp.maximum(all_counts, 1.0)[:, None]
    return (tile_power, sky_power)


def solution(mesh):
    in_specs = (
        P("ra", "dec", None, None),
        P("ra", "dec", None),
        P("ra", "dec", None, None),
        P("ra", "dec", None, None),
        P("ra", "dec"),
        P("ra", "dec", None, None, None),
    )
    out_specs = (P("ra", "dec", None, None), P())
    return jax.shard_map(
        per_device, mesh=mesh, in_specs=in_specs, out_specs=out_specs, check_vma=False
    )
```

profile of v0, /device:TPU:0, one launch (start us, length us, event | category | flops | bytes accessed | tf_op | source)
XLA Modules:
  0.0 456.6 jit_solution(12260927048021557537)
XLA Ops:
  0.7 8.5 %sine_convert_fusion = (bf16[1024,512]{1,0:T(8,128)(2,1)S(1)}, bf16[1024,512]{1,0:T(8,128)(2,1)S(1)}) fusion(), kind=kLoop, calls=%fused_computation.29 | loop fusion | flops 8388608 | bytes 2097152 | tf_op jit(solution)/shard_map/convert.2
  9.2 2.9 multiply_convert_fusion
  12.2 2.4 collective-permute-start
  16.1 4.4 collective-permute-done.1
  23.2 28.7 %collective-permute-done.2 = bf16[1,6,128,1024]{3,2,1,0:T(8,128)(2,1)} collective-permute-done((bf16[1,6,128,1024]{3,2,1,0:T(8,128)(2,1)}, bf16[1,6,128,1024]{3,2,1,0:T(8,128)(2,1)}, u32[]{:S(2)}, u32[]{:S(2)}) %collective-permute-start.2) | collective-permute-done | bytes 1572896 | tf_op jit(solution)/shard_map/ppermute | solution.py:26
  51.8 3.6 pad_maximum_fusion
  55.4 343.0 %while.14 = (s32[]{:T(128)}, f32[8,1024]{1,0:T(8,128)S(1)}, f32[8]{0:T(128)S(1)}, s32[]{:T(128)}, s32[40,128,128]{2,1,0:T(8,128)}, /*index=5*/s32[40,3]{0,1:T(4,...) while((s32[]{:T(128)}, f32[8,1024]{1,0:T(8,128)S(1)}, ...), condition=%wide.region_3.4_spmd, body=%wide.region_0.3_spmd.sunk | while | flops 271319072 | bytes 2032330 | solution.py:105
  89.5 1.7 multiply_reduce_fusion.2
  98.5 1.7 multiply_reduce_fusion.2
  107.5 1.7 multiply_reduce_fusion.2
  143.5 1.7 multiply_reduce_fusion.2
  161.5 1.7 multiply_reduce_fusion.2
  170.6 1.7 multiply_reduce_fusion.2
  179.6 1.7 multiply_reduce_fusion.2
  215.6 1.7 multiply_reduce_fusion.2
  233.6 1.7 multiply_reduce_fusion.2
  242.6 1.7 multiply_reduce_fusion.2
  251.6 1.7 multiply_reduce_fusion.2
  287.7 1.7 multiply_reduce_fusion.2
  305.7 1.7 multiply_reduce_fusion.2
  314.7 1.7 multiply_reduce_fusion.2
  323.7 1.7 multiply_reduce_fusion.2
  359.8 1.7 multiply_reduce_fusion.2
  399.4 56.5 %all-reduce = (f32[8,128]{1,0:T(8,128)S(1)}, f32[8]{0:T(128)S(1)}) all-reduce(f32[8,128]{1,0:T(8,128)S(1)} %fusion.21, f32[8]{0:T(128)S(1)} %get-tuple-element.99), channel_id=1, replica_groups=mesh['ra'=4,'dec'=8] {'ra','dec'}, use_global_device_ids=true, to_apply=%region_4.5 | all-reduce | flops 1032 | bytes 8256 | tf_op jit(solution)/shard_map/psum | solution.py:108
  (312 shorter events, 148.2 us)
Async XLA Ops:
  0.6 8.5 %copy-start = (s32[2,4,2,128]{3,2,1,0:T(2,128)S(1)}, s32[2,4,2,128]{3,2,1,0:T(2,128)}, u32[]{:S(2)}) copy-start(s32[2,4,2,128]{3,2,1,0:T(2,128)} %param.10) | copy-start | bytes 24580
  0.6 8.6 %copy-start.2 = (bf16[2,4,128,1024]{3,2,1,0:T(8,128)(2,1)S(1)}, bf16[2,4,128,1024]{3,2,1,0:T(8,128)(2,1)}, u32[]{:S(2)}) copy-start(bf16[2,4,128,1024]{3,2,1,0:T(8,128)(2,1)} %param.8) | copy-start | bytes 6291460
  0.6 8.6 %copy-start.3 = (f32[2,4,128]{2,1,0:T(4,128)S(1)}, f32[2,4,128]{2,1,0:T(4,128)}, u32[]{:S(2)}) copy-start(f32[2,4,128]{2,1,0:T(4,128)} %param.9) | copy-start | bytes 12292
  12.2 3.9 collective-permute-start
  14.6 8.5 %copy-start.1 = (s32[1,1,40,3]{2,1,3,0:T(1,128)S(1)}, s32[1,1,40,3]{2,1,3,0:T(1,128)}, u32[]{:S(2)}) copy-start(s32[1,1,40,3]{2,1,3,0:T(1,128)} %param.11) | copy-start | bytes 1444
  14.6 5.9 %collective-permute-start.1 = (bf16[2,1,128,1024]{3,2,1,0:T(8,128)(2,1)S(1)}, bf16[2,1,128,1024]{3,2,1,0:T(8,128)(2,1)S(1)}, u32[]{:S(2)}, u32[]{:S(2)}) collective-permute-start(bf16[2,1,128,1024]{3,2,1,0:T(8,128)(2,1)S(1)} %get-tuple-element.122), channel_id=1, source_target_pairs={{1,0},{2,1},{3,2},{4,3},{5,4},{6,5},{7,6},{9,8},{10,9},{11,10},{12... | collective-permute-start | bytes 1572872 | tf_op jit(solution)/shard_map/ppermute | solution.py:18
  21.8 30.0 %collective-permute-start.2 = (bf16[1,6,128,1024]{3,2,1,0:T(8,128)(2,1)}, bf16[1,6,128,1024]{3,2,1,0:T(8,128)(2,1)}, u32[]{:S(2)}, u32[]{:S(2)}) collective-permute-start(bf16[1,6,128,1024]{3,2,1,0:T(8,128)(2,1)} %pad_maximum_fusion.1), channel_id=1, source_target_pairs={{8,0},{16,8},{24,16},{9,1},{17,9},{25,17},{10,2},{18,10},{26,18},{... | collective-permute-start | bytes 4718600 | tf_op jit(solution)/shard_map/ppermute | solution.py:26
where the time goes:
time: 464 us; the launch traced here: 457 us
  loops' own time  174 us (38%)
  matrix products  66.7 us (14%)
  other arithmetic  62.7 us (14%)
  local copies, waits for them, and re-layouts  57.8 us (12%)
  blocking collectives  56.5 us (12%)
  waiting for transfers between devices  33.2 us (7%)
  starting transfers between devices  5 us (1%)
    another operation x1, loops' own time, per_device(): sums, counts = lax.fori_loop(0, live_count, add_live, start_value)  174 us
    dot_general x38, matrix products, block_term(): jnp.dot(onehot.reshape(n_sep * per_cell, per_cell), right, preferred_elem...  63.4 us
    psum x1, blocking collectives, per_device(): summed, all_counts = lax.psum((binned, counts), ('ra', 'dec'))  56.5 us
    mul x38, other arithmetic, block_term(): block_sum = jnp.sum(mixed * left.astype(jnp.float32)[None], axis=1)  37.8 us
    eq x38, local copies, waits for them, and re-layouts, block_term(): sep_bins[None, :, :] == jnp.arange(n_sep, dtype=jnp.int32)[:, None, None]  32.5 us
    ppermute x1, waiting for transfers between devices, from_behind(): lax.ppermute(value, axis, [(source, source + steps) for source in range(l...  28.7 us
    slice x38, local copies, waits for them, and re-layouts, slot_term(): index_b = (row_a + entry_row[1]) * cols_pad + col_a + entry_row[2]  22.3 us
    reduce_sum x38, other arithmetic, block_term(): pair_counts = jnp.sum(onehot.reshape(n_sep, -1).astype(jnp.float32), axis=1)  9.44 us
  transfers between devices with their start and end apart: 3, of which 3 were waited for; matrix products, arithmetic and copies ran while one was open for 0% of the time, Pallas kernels for 0%

commit v1 on v0

--- a/solution.py
+++ b/solution.py
@@ -105,7 +105,7 @@
     sums, counts = lax.fori_loop(0, live_count, add_live, start_value)
     binned = jnp.dot(sums, kbin_table(length // 2, NKB), precision=lax.Precision.HIGHEST)
     tile_power = (binned / (per_cell * length)).reshape(1, 1, NSEP, NKB)
-    summed, all_counts = lax.psum((binned, counts), ("ra", "dec"))
+    summed, all_counts = lax.psum(lax.psum((binned, counts), "ra"), "dec")
     sky_power = summed / jnp.maximum(all_counts, 1.0)[:, None]
     return (tile_power, sky_power)
 

time: 464 us -> 444 us (0.957)
  blocking collectives: 56.5 us -> 39 us
    psum x1 -> x2, blocking collectives: 56.5 us -> 39 us  [per_device(): summed, all_counts = lax.psum(lax.psum((binned, counts), 'ra'), 'dec')]
where the time goes in v1:
time: 444 us; the launch traced here: 437 us
  loops' own time  172 us (39%)
  matrix products  66.6 us (15%)
  other arithmetic  62.7 us (14%)
  local copies, waits for them, and re-layouts  57.1 us (13%)
  blocking collectives  39 us (9%)
  waiting for transfers between devices  33.2 us (7%)
  starting transfers between devices  5 us (1%)
    another operation x1, loops' own time, per_device(): sums, counts = lax.fori_loop(0, live_count, add_live, start_value)  172 us
    dot_general x38, matrix products, block_term(): jnp.dot(onehot.reshape(n_sep * per_cell, per_cell), right, preferred_elem...  63.4 us
    psum x2, blocking collectives, per_device(): summed, all_counts = lax.psum(lax.psum((binned, counts), 'ra'), 'dec')  39 us
    mul x38, other arithmetic, block_term(): block_sum = jnp.sum(mixed * left.astype(jnp.float32)[None], axis=1)  37.8 us
    eq x38, local copies, waits for them, and re-layouts, block_term(): sep_bins[None, :, :] == jnp.arange(n_sep, dtype=jnp.int32)[:, None, None]  32.5 us
    ppermute x1, waiting for transfers between devices, from_behind(): lax.ppermute(value, axis, [(source, source + steps) for source in range(l...  28.7 us
    slice x38, local copies, waits for them, and re-layouts, slot_term(): index_b = (row_a + entry_row[1]) * cols_pad + col_a + entry_row[2]  21.6 us
    reduce_sum x38, other arithmetic, block_term(): pair_counts = jnp.sum(onehot.reshape(n_sep, -1).astype(jnp.float32), axis=1)  9.44 us
  transfers between devices with their start and end apart: 3, of which 3 were waited for; matrix products, arithmetic and copies ran while one was open for 0% of the time, Pallas kernels for 0%

profile of v1, /device:TPU:0, one launch (start us, length us, event | category | flops | bytes accessed | tf_op | source)
XLA Modules:
  0.0 436.9 jit_solution(6939876547717823608)
XLA Ops:
  0.7 8.5 %sine_convert_fusion = (bf16[1024,512]{1,0:T(8,128)(2,1)S(1)}, bf16[1024,512]{1,0:T(8,128)(2,1)S(1)}) fusion(), kind=kLoop, calls=%fused_computation.29 | loop fusion | flops 8388608 | bytes 2097152 | tf_op jit(solution)/shard_map/convert.2
  9.2 2.9 multiply_convert_fusion
  12.2 2.4 collective-permute-start
  16.1 4.4 %collective-permute-done.1 = bf16[2,1,128,1024]{3,2,1,0:T(8,128)(2,1)S(1)} collective-permute-done((bf16[2,1,128,1024]{3,2,1,0:T(8,128)(2,1)S(1)}, bf16[2,1,128,1024]{3,2,1,0:T(8,128)(2,1)S(1)}, u32[]{:S(2)}, u32[]{:S(2)}) %collective-permute-start.1) | collective-permute-done | bytes 524320 | tf_op jit(solution)/shard_map/ppermute | solution.py:18
  23.2 28.7 %collective-permute-done.2 = bf16[1,6,128,1024]{3,2,1,0:T(8,128)(2,1)} collective-permute-done((bf16[1,6,128,1024]{3,2,1,0:T(8,128)(2,1)}, bf16[1,6,128,1024]{3,2,1,0:T(8,128)(2,1)}, u32[]{:S(2)}, u32[]{:S(2)}) %collective-permute-start.2) | collective-permute-done | bytes 1572896 | tf_op jit(solution)/shard_map/ppermute | solution.py:26
  51.8 3.6 pad_maximum_fusion
  55.4 340.8 %while.14 = (s32[]{:T(128)}, f32[8,1024]{1,0:T(8,128)S(1)}, f32[8]{0:T(128)S(1)}, s32[]{:T(128)}, s32[40,128,128]{2,1,0:T(8,128)}, /*index=5*/s32[40,3]{0,1:T(4,...) while((s32[]{:T(128)}, f32[8,1024]{1,0:T(8,128)S(1)}, ...), condition=%wide.region_3.4_spmd, body=%wide.region_0.3_spmd.sunk | while | flops 271319072 | bytes 2032330 | solution.py:105
  62.4 1.7 multiply_reduce_fusion.2
  71.4 1.7 multiply_reduce_fusion.2
  80.3 1.7 multiply_reduce_fusion.2
  89.3 1.7 multiply_reduce_fusion.2
  98.2 1.7 multiply_reduce_fusion.2
  107.2 1.7 multiply_reduce_fusion.2
  116.1 1.7 multiply_reduce_fusion.2
  125.1 1.7 multiply_reduce_fusion.2
  134.0 1.7 multiply_reduce_fusion.2
  143.0 1.7 multiply_reduce_fusion.2
  151.9 1.7 multiply_reduce_fusion.2
  160.9 1.7 multiply_reduce_fusion.2
  169.8 1.7 multiply_reduce_fusion.2
  178.8 1.7 multiply_reduce_fusion.2
  250.4 1.7 multiply_reduce_fusion.2
  397.2 8.5 %all-reduce.1 = (f32[8,128]{1,0:T(8,128)S(1)}, f32[8]{0:T(128)S(1)}) all-reduce(f32[8,128]{1,0:T(8,128)S(1)} %fusion.21, f32[8]{0:T(128)S(1)} %get-tuple-element.99), channel_id=1, replica_groups=mesh['ra'=4,'dec'=8] {'ra'}, use_global_device_ids=true, to_apply=%region_4.5 | all-reduce | flops 1032 | bytes 8256 | tf_op jit(solution)/shard_map/psum | solution.py:108
  405.7 30.5 %all-reduce = (f32[8,128]{1,0:T(8,128)S(1)}, f32[8]{0:T(128)S(1)}) all-reduce(f32[8,128]{1,0:T(8,128)S(1)} %get-tuple-element.116, f32[8]{0:T(128)S(1)} %get-tuple-element.117), channel_id=1, replica_groups=mesh['ra'=4,'dec'=8] {'dec'}, use_global_device_ids=true, to_apply=%region_5.6 | all-reduce | flops 1032 | bytes 8256 | tf_op jit(solution)/shard_map/psum | solution.py:108
  (313 shorter events, 149.2 us)
Async XLA Ops:
  0.6 8.5 %copy-start = (s32[2,4,2,128]{3,2,1,0:T(2,128)S(1)}, s32[2,4,2,128]{3,2,1,0:T(2,128)}, u32[]{:S(2)}) copy-start(s32[2,4,2,128]{3,2,1,0:T(2,128)} %param.10) | copy-start | bytes 24580
  0.6 8.6 %copy-start.2 = (bf16[2,4,128,1024]{3,2,1,0:T(8,128)(2,1)S(1)}, bf16[2,4,128,1024]{3,2,1,0:T(8,128)(2,1)}, u32[]{:S(2)}) copy-start(bf16[2,4,128,1024]{3,2,1,0:T(8,128)(2,1)} %param.8) | copy-start | bytes 6291460
  0.6 8.6 %copy-start.3 = (f32[2,4,128]{2,1,0:T(4,128)S(1)}, f32[2,4,128]{2,1,0:T(4,128)}, u32[]{:S(2)}) copy-start(f32[2,4,128]{2,1,0:T(4,128)} %param.9) | copy-start | bytes 12292
  12.2 3.9 collective-permute-start
  14.6 8.5 %copy-start.1 = (s32[1,1,40,3]{2,1,3,0:T(1,128)S(1)}, s32[1,1,40,3]{2,1,3,0:T(1,128)}, u32[]{:S(2)}) copy-start(s32[1,1,40,3]{2,1,3,0:T(1,128)} %param.11) | copy-start | bytes 1444
  14.6 5.9 %collective-permute-start.1 = (bf16[2,1,128,1024]{3,2,1,0:T(8,128)(2,1)S(1)}, bf16[2,1,128,1024]{3,2,1,0:T(8,128)(2,1)S(1)}, u32[]{:S(2)}, u32[]{:S(2)}) collective-permute-start(bf16[2,1,128,1024]{3,2,1,0:T(8,128)(2,1)S(1)} %get-tuple-element.124), channel_id=1, source_target_pairs={{1,0},{2,1},{3,2},{4,3},{5,4},{6,5},{7,6},{9,8},{10,9},{11,10},{12... | collective-permute-start | bytes 1572872 | tf_op jit(solution)/shard_map/ppermute | solution.py:18
  21.9 30.0 %collective-permute-start.2 = (bf16[1,6,128,1024]{3,2,1,0:T(8,128)(2,1)}, bf16[1,6,128,1024]{3,2,1,0:T(8,128)(2,1)}, u32[]{:S(2)}, u32[]{:S(2)}) collective-permute-start(bf16[1,6,128,1024]{3,2,1,0:T(8,128)(2,1)} %pad_maximum_fusion.1), channel_id=1, source_target_pairs={{8,0},{16,8},{24,16},{9,1},{17,9},{25,17},{10,2},{18,10},{26,18},{... | collective-permute-start | bytes 4718600 | tf_op jit(solution)/shard_map/ppermute | solution.py:26
